TPU v7x, 32 devices: a whole 2x2x4 slice. The times are simulated.
32 devices in a mesh: row: 4 (over x, core), col: 8 (over z, y).
Axes of the slice: x: 2, y: 2, z: 4, core: 2. Of those that a mesh axis runs over, the one named last changes fastest.
Arguments:
- vectors: bfloat16 [1, 16, 4096], P(None, None, ('col', 'row')), may hold values from -110 to 110
- h_tiles: bfloat16 [1, 4, 256, 128, 128], P(None, 'row', 'col'), may hold values from -0.15625 to 0.15625
- h_list: int32 [1, 4, 256], P(None, 'row', 'col'), may hold values from -1 to 31, as said below
- j_tiles: bfloat16 [1, 4, 96, 128, 128], P(None, 'row', 'col'), may hold values from -0.25 to 0.25
- j_list: int32 [1, 4, 96], P(None, 'row', 'col'), may hold values from -1 to 63, as said below
Outputs:
- basis: float32 [1, 16, 4096], P(None, None, ('row', 'col'))
- transitions: float32 [1, 2, 16, 16], replicated
Inputs may be any that keep to these rules, and one draw needn't show every extreme that they name: `h_list`: each block's 32 entries list distinct tile positions first and then -1; at most 32 positions a block, and some block lists all 32. `j_list`: each block's 12 entries list distinct codes first and then -1; at most 12 codes a block, and some block lists all 12.
All inputs are finite; a program needn't handle non-finite values.
Results may differ from a plain program's by a relative error of at most 0.0003.
Values may be sent and summed in bfloat16 or wider, within the bound.
No kernel may reach another device: no remote copies, remote signals or barrier semaphores. Data moves between devices by JAX's collectives and lax.ppermute only.
A program may use at most 64 MiB of HBM per device.

v0:
```python
import math
import jax
import jax.numpy as jnp
from jax import lax
from jax.sharding import PartitionSpec as P

NSIT = 6
exact_precision = lax.Precision.HIGHEST


def local_product(tile_data, code_data, vector_block, operator_count, row_tiles):
    sector_count = tile_data.shape[0]
    tile_size = tile_data.shape[2]
    vector_count = vector_block.shape[1]
    column_tiles = vector_block.shape[2] // tile_size
    position_count = row_tiles * column_tiles
    column_vectors = vector_block.reshape(sector_count, vector_count, column_tiles, tile_size)
    places = code_data % position_count
    operator = code_data // position_count
    column_hot = (
        places[:, :, None] % column_tiles == jnp.arange(column_tiles)[None, None, :]
    ).astype(jnp.bfloat16)
    picked = jnp.einsum(
        "sqc,skcb->sqkb", column_hot, column_vectors, preferred_element_type=jnp.float32
    ).astype(jnp.bfloat16)
    product = jnp.einsum("sqab,sqkb->sqka", tile_data, picked, preferred_element_type=jnp.float32)
    row_hot = (
        (operator[:, :, None, None] == jnp.arange(operator_count)[None, None, :, None])
        & (places[:, :, None, None] // column_tiles == jnp.arange(row_tiles)[None, None, None, :])
        & (code_data[:, :, None, None] >= 0)
    ).astype(jnp.float32)
    result = jnp.einsum("sqor,sqka->sokra", row_hot, product, precision=exact_precision)
    return result.reshape(sector_count, operator_count * vector_count, row_tiles * tile_size)


def inverse_root_of(gram, vector_count):
    scale = jnp.sqrt(jnp.sum(gram * gram, axis=(1, 2), keepdims=True) + 1e-06)
    iterate = gram / scale
    identity = jnp.eye(vector_count, dtype=jnp.float32)[None]
    inverse_root = identity
    for iteration in range(NSIT):
        middle = 1.5 * identity - 0.5 * jnp.einsum(
            "skm,sml->skl", inverse_root, iterate, precision=exact_precision
        )
        iterate = jnp.einsum("skm,sml->skl", iterate, middle, precision=exact_precision)
        inverse_root = jnp.einsum("skm,sml->skl", middle, inverse_root, precision=exact_precision)
    return (inverse_root, scale)


def per_device(vectors, h_tiles, h_list, j_tiles, j_list):
    sector_count = vectors.shape[0]
    vector_count = vectors.shape[1]
    tile_size = h_tiles.shape[-1]
    block_rows = vectors.shape[2] * lax.axis_size("col")
    total_rows = block_rows * lax.axis_size("row")
    row_tiles = block_rows // tile_size
    vector_block = lax.all_gather(vectors, "row", axis=2, tiled=True)
    h_part = local_product(
        h_tiles.reshape(sector_count, -1, tile_size, tile_size),
        h_list.reshape(sector_count, -1),
        vector_block,
        1,
        row_tiles,
    )
    j_part = local_product(
        j_tiles.reshape(sector_count, -1, tile_size, tile_size),
        j_list.reshape(sector_count, -1),
        vector_block,
        2,
        row_tiles,
    )
    projected, applied = (
        lax.psum_scatter(h_part, "col", scatter_dimension=2, tiled=True),
        lax.psum_scatter(j_part, "col", scatter_dimension=2, tiled=True),
    )
    gram_part = jnp.einsum("skp,slp->skl", projected, projected, precision=exact_precision)
    gram = lax.psum(gram_part, ("row", "col"))
    inverse_root, scale = inverse_root_of(gram, vector_count)
    basis = jnp.sqrt(total_rows / scale) * jnp.einsum(
        "smk,smp->skp", inverse_root, projected, precision=exact_precision
    )
    element_part = jnp.einsum("skp,smp->skm", basis, applied, precision=exact_precision)
    elements = lax.psum(element_part, ("row", "col")) / math.sqrt(total_rows)
    elements = elements.reshape(sector_count, vector_count, 2, vector_count).transpose(0, 2, 1, 3)
    return (basis, elements)


def solution(mesh):
    return jax.shard_map(
        per_device,
        mesh=mesh,
        in_specs=(
            P(None, None, ("col", "row")),
            P(None, "row", "col", None, None),
            P(None, "row", "col"),
            P(None, "row", "col", None, None),
            P(None, "row", "col"),
        ),
        out_specs=(P(None, None, ("row", "col")), P()),
        check_vma=False,
    )
```

profile of v0, /device:TPU:0, one launch (start us, length us, event | category | flops | bytes accessed | tf_op | source)
XLA Modules:
  0.0 189.2 jit_solution(17668249501114527060)
XLA Ops:
  7.2 0.0 copy-start
  7.2 0.0 reduce-scatter.5.cloned.1.call-start
  7.2 0.7 fusion.38
  8.0 6.4 %all_gather.3 = bf16[1,16,512]{2,1,0:T(8,128)(2,1)S(1)} all-gather(bf16[1,16,128]{2,1,0:T(8,128)(2,1)} %param.5), channel_id=1, replica_groups=mesh['row'=4,'col'=8] {'row'}, dimensions={2}, use_global_device_ids=true | all-gather | bytes 20480 | tf_op jit(solution)/shard_map/all_gather | solution.py:57
  14.4 0.2 convolution_convert_fusion
  14.6 0.0 copy-done
  14.7 0.6 fusion.6
  15.3 0.3 convolution_bitcast_fusion.2
  15.6 0.6 reshape.796
  16.2 0.0 reduce-scatter.5.cloned.1.call-update
  16.3 0.0 reduce-scatter.7.cloned.1.call-start
  16.3 0.7 bitcast_compare_fusion
  17.0 0.7 and_select_fusion.1
  17.7 0.2 convolution_convert_fusion.1
  17.9 1.3 convolution_bitcast_fusion.1
  19.2 0.3 convolution_bitcast_fusion
  19.5 13.7 %copy.19 = f32[1,32,1024]{0,1,2:T(8,128)} copy(f32[1,32,1024]{2,0,1:T(1,128)S(1)} %bitcast.122) | data formatting | bytes 262144
  33.2 9.0 %bitcast_reduce_fusion = f32[1024,32]{1,0:T(8,128)} fusion(f32[1,32,1024]{0,1,2:T(8,128)} %copy.19), kind=kLoop, calls=%fused_computation | loop fusion | bytes 262144
  42.2 0.0 reduce-scatter.7.cloned.1.call-update
  42.2 30.7 %reduce-scatter.5.cloned.1.call-done = f32[1,16,128]{2,1,0:T(8,128)} async-done(((f32[1,16,1024]{2,1,0:T(8,128)}), f32[1,16,128]{2,1,0:T(8,128)}) %reduce-scatter.5.cloned.1.call-update) | async-done | bytes 8208 | tf_op jit(solution)/shard_map/reduce_scatter | solution.py:73
  72.9 0.9 convolution_bitcast_fusion.4
  73.8 40.3 %psum.14 = f32[1,16,16]{2,1,0:T(8,128)S(1)} all-reduce(f32[1,16,16]{2,1,0:T(8,128)S(1)} %convolution_bitcast_fusion.4), channel_id=1, replica_groups=mesh['row'=4,'col'=8] {'row','col'}, use_global_device_ids=true, to_apply=%region_1.2 | all-reduce | flops 256 | bytes 2048 | tf_op jit(solution)/shard_map/psum | solution.py:77
  114.2 0.6 multiply_reduce_fusion
  115.5 0.1 fusion.5
  115.6 0.1 fusion.13
  115.7 0.1 fusion.18
  115.9 0.1 fusion.4
  116.0 0.1 fusion.40
  116.1 0.1 fusion.39
  116.3 0.1 fusion.3
  116.4 0.1 fusion.42
  116.6 0.1 fusion.41
  116.7 0.1 fusion.2
  116.8 0.1 fusion.44
  117.0 0.1 fusion.43
  117.1 0.1 fusion.1
  117.3 0.1 fusion.45
  117.4 0.1 fusion.46
  117.5 0.1 fusion
  117.7 0.1 fusion.47
  117.9 0.9 convolution_multiply_fusion
  118.8 0.0 copy-start.1
  118.8 19.9 %reduce-scatter.7.cloned.1.call-done = f32[128,32]{1,0:T(8,128)} async-done(((f32[1024,32]{1,0:T(8,128)}), f32[128,32]{1,0:T(8,128)}) %reduce-scatter.7.cloned.1.call-update) | async-done | bytes 16400
  138.7 1.4 reshape_bitcast_fusion
  140.2 1.3 copy.20
  141.5 0.1 convolution_bitcast_fusion.3
  141.6 40.0 %psum.15 = f32[1,16,32]{2,1,0:T(8,128)S(1)} all-reduce(f32[1,16,32]{2,1,0:T(8,128)S(1)} %convolution_bitcast_fusion.3), channel_id=1, replica_groups=mesh['row'=4,'col'=8] {'row','col'}, use_global_device_ids=true, to_apply=%region_4.5 | all-reduce | flops 512 | bytes 4096 | tf_op jit(solution)/shard_map/psum | solution.py:83
  181.7 0.1 reshape.803
  181.7 0.6 copy.30
  182.3 0.0 copy-done.1
  (9 shorter events, 0.1 us)
Async XLA Ops:
  7.2 7.5 %copy-start = (bf16[1,1,32,128,128]{4,3,2,1,0:T(8,128)(2,1)S(1)}, bf16[1,1,32,128,128]{4,3,2,1,0:T(8,128)(2,1)}, u32[]{:S(2)}) copy-start(bf16[1,1,32,128,128]{4,3,2,1,0:T(8,128)(2,1)} %param.6) | copy-start | bytes 3145732
  7.2 65.8 %reduce-scatter.5.cloned.1.call-start = ((), (), s32[]{:S(2)}) async-start(), calls=%async_computation.2 | async-start | bytes 73728 | tf_op jit(solution)/shard_map/reduce_scatter | solution.py:73
  16.3 122.5 %reduce-scatter.7.cloned.1.call-start = ((), (), s32[]{:S(2)}) async-start(), calls=%async_computation.3 | async-start | bytes 589824
  118.8 63.5 %copy-start.1 = (f32[16,128]{1,0:T(8,128)}, f32[16,128]{1,0:T(8,128)S(1)}, u32[]{:S(2)}) copy-start(f32[16,128]{1,0:T(8,128)S(1)} %convolution_multiply_fusion) | copy-start | bytes 24580
Sparse Core Ops, SparseCore 0:
  16.4 56.5 reduce-scatter.4
  76.3 62.3 reduce-scatter.6
where the time goes:
time: 190 us; the launch traced here: 189 us
  blocking collectives  86.8 us (46%)
  waiting for transfers between devices  50.7 us (27%)
  local copies, waits for them, and re-layouts  26.9 us (14%)
  between operations  14.9 us (8%)
  matrix products  7.18 us (4%)
  other arithmetic  2.72 us (1%)
    psum x1, blocking collectives, per_device(): gram = lax.psum(gram_part, ('row', 'col'))  40.3 us
    psum x1, blocking collectives, per_device(): elements = lax.psum(element_part, ('row', 'col')) / math.sqrt(total_rows)  40 us
    reduce_scatter x1, waiting for transfers between devices, per_device(): lax.psum_scatter(h_part, 'col', scatter_dimension=2, tiled=True)  30.7 us
    unnamed x8, local copies, waits for them, and re-layouts  25.5 us
    unnamed x3, waiting for transfers between devices  20 us
    all_gather x1, blocking collectives, per_device(): vector_block = lax.all_gather(vectors, 'row', axis=2, tiled=True)  6.39 us
  transfers between devices with their start and end apart: 2, of which 2 were waited for; matrix products, arithmetic and copies ran while one was open for 16% of the time, Pallas kernels for 0%

commit v1 on v0

--- a/solution.py
+++ b/solution.py
@@ -80,7 +80,7 @@
         "smk,smp->skp", inverse_root, projected, precision=exact_precision
     )
     element_part = jnp.einsum("skp,smp->skm", basis, applied, precision=exact_precision)
-    elements = lax.psum(element_part, ("row", "col")) / math.sqrt(total_rows)
+    elements = jnp.sum(lax.all_gather(element_part, ("row", "col")), axis=0) / math.sqrt(total_rows)
     elements = elements.reshape(sector_count, vector_count, 2, vector_count).transpose(0, 2, 1, 3)
     return (basis, elements)
 

time: 190 us -> 216 us (1.14)
  blocking collectives: 86.8 us -> 113 us
    all_gather x0 -> x1, blocking collectives: none -> 66 us  [per_device(): lax.all_gather(element_part, ('row', 'col'))]
    psum x1 -> x0, blocking collectives: 40 us -> none  [per_device(): elements = lax.psum(element_part, ('row', 'col')) / math.sqrt(total_rows)]
    unnamed x8 -> x9, local copies, waits for them, and re-layouts: 25.5 us -> 26.1 us
  transfers between devices with their start and end apart: 2 -> 2, of which waited for: 2 -> 2; matrix products, arithmetic and copies ran while one was open for 16% -> 14% of each run, Pallas kernels for 0% -> 0%
where the time goes in v1:
time: 216 us; the launch traced here: 215 us
  blocking collectives  113 us (52%)
  waiting for transfers between devices  50.7 us (23%)
  local copies, waits for them, and re-layouts  26.9 us (12%)
  between operations  14.9 us (7%)
  matrix products  7.18 us (3%)
  other arithmetic  2.76 us (1%)
    all_gather x1, blocking collectives, per_device(): lax.all_gather(element_part, ('row', 'col'))  66 us
    psum x1, blocking collectives, per_device(): gram = lax.psum(gram_part, ('row', 'col'))  40.3 us
    reduce_scatter x1, waiting for transfers between devices, per_device(): lax.psum_scatter(h_part, 'col', scatter_dimension=2, tiled=True)  30.7 us
    unnamed x9, local copies, waits for them, and re-layouts  26.1 us
    unnamed x3, waiting for transfers between devices  20 us
    all_gather x1, blocking collectives, per_device(): vector_block = lax.all_gather(vectors, 'row', axis=2, tiled=True)  6.39 us
  transfers between devices with their start and end apart: 2, of which 2 were waited for; matrix products, arithmetic and copies ran while one was open for 14% of the time, Pallas kernels for 0%

profile of v1, /device:TPU:0, one launch (start us, length us, event | category | flops | bytes accessed | tf_op | source)
XLA Modules:
  0.0 215.2 jit_solution(10224163436881815991)
XLA Ops:
  7.2 0.0 copy-start
  7.2 0.0 reduce-scatter.5.cloned.1.call-start
  7.2 0.7 fusion.38
  8.0 6.4 %all_gather.9 = bf16[1,16,512]{2,1,0:T(8,128)(2,1)S(1)} all-gather(bf16[1,16,128]{2,1,0:T(8,128)(2,1)} %param.5), channel_id=1, replica_groups=mesh['row'=4,'col'=8] {'row'}, dimensions={2}, use_global_device_ids=true | all-gather | bytes 20480 | tf_op jit(solution)/shard_map/all_gather | solution.py:57
  14.4 0.2 convolution_convert_fusion
  14.6 0.0 copy-done
  14.7 0.6 fusion.6
  15.3 0.3 convolution_bitcast_fusion.2
  15.6 0.6 reshape.811
  16.2 0.0 reduce-scatter.5.cloned.1.call-update
  16.3 0.0 reduce-scatter.7.cloned.1.call-start
  16.3 0.7 bitcast_compare_fusion
  17.0 0.7 and_select_fusion.1
  17.7 0.2 convolution_convert_fusion.1
  17.9 1.3 convolution_bitcast_fusion.1
  19.2 0.3 convolution_bitcast_fusion
  19.5 13.7 %copy.18 = f32[1,32,1024]{0,1,2:T(8,128)} copy(f32[1,32,1024]{2,0,1:T(1,128)S(1)} %bitcast.120) | data formatting | bytes 262144
  33.2 9.0 %bitcast_reduce_fusion = f32[1024,32]{1,0:T(8,128)} fusion(f32[1,32,1024]{0,1,2:T(8,128)} %copy.18), kind=kLoop, calls=%fused_computation | loop fusion | bytes 262144
  42.2 0.0 reduce-scatter.7.cloned.1.call-update
  42.2 30.7 %reduce-scatter.5.cloned.1.call-done = f32[1,16,128]{2,1,0:T(8,128)} async-done(((f32[1,16,1024]{2,1,0:T(8,128)}), f32[1,16,128]{2,1,0:T(8,128)}) %reduce-scatter.5.cloned.1.call-update) | async-done | bytes 8208 | tf_op jit(solution)/shard_map/reduce_scatter | solution.py:73
  72.9 0.9 convolution_bitcast_fusion.3
  73.8 40.3 %psum.7 = f32[1,16,16]{2,1,0:T(8,128)S(1)} all-reduce(f32[1,16,16]{2,1,0:T(8,128)S(1)} %convolution_bitcast_fusion.3), channel_id=1, replica_groups=mesh['row'=4,'col'=8] {'row','col'}, use_global_device_ids=true, to_apply=%region_1.2 | all-reduce | flops 256 | bytes 2048 | tf_op jit(solution)/shard_map/psum | solution.py:77
  114.2 0.6 multiply_reduce_fusion
  115.5 0.1 fusion.5
  115.6 0.1 fusion.13
  115.7 0.1 fusion.18
  115.9 0.1 fusion.4
  116.0 0.1 fusion.40
  116.1 0.1 fusion.39
  116.3 0.1 fusion.3
  116.4 0.1 fusion.42
  116.6 0.1 fusion.41
  116.7 0.1 fusion.2
  116.8 0.1 fusion.44
  117.0 0.1 fusion.43
  117.1 0.1 fusion.1
  117.3 0.1 fusion.45
  117.4 0.1 fusion.46
  117.5 0.1 fusion
  117.7 0.1 fusion.47
  117.9 0.9 convolution_multiply_fusion
  118.8 0.0 copy-start.1
  118.8 19.9 %reduce-scatter.7.cloned.1.call-done = f32[128,32]{1,0:T(8,128)} async-done(((f32[1024,32]{1,0:T(8,128)}), f32[128,32]{1,0:T(8,128)}) %reduce-scatter.7.cloned.1.call-update) | async-done | bytes 16400
  138.7 1.4 reshape_bitcast_fusion
  140.2 1.3 copy.19
  141.5 0.1 fusion.48
  141.6 66.0 %all-gather = f32[512,32]{1,0:T(8,128)S(1)} all-gather(f32[16,32]{1,0:T(8,128)S(1)} %fusion.48), channel_id=2, replica_groups=mesh['row'=4,'col'=8] {'row','col'}, dimensions={0}, use_global_device_ids=true | all-gather | bytes 67584 | tf_op jit(solution)/shard_map/all_gather | solution.py:83
  207.6 0.1 div.89
  207.7 0.6 copy.14
  208.3 0.0 copy-done.1
  (10 shorter events, 0.1 us)
Async XLA Ops:
  7.2 7.5 %copy-start = (bf16[1,1,32,128,128]{4,3,2,1,0:T(8,128)(2,1)S(1)}, bf16[1,1,32,128,128]{4,3,2,1,0:T(8,128)(2,1)}, u32[]{:S(2)}) copy-start(bf16[1,1,32,128,128]{4,3,2,1,0:T(8,128)(2,1)} %param.6) | copy-start | bytes 3145732
  7.2 65.8 %reduce-scatter.5.cloned.1.call-start = ((), (), s32[]{:S(2)}) async-start(), calls=%async_computation.2 | async-start | bytes 73728 | tf_op jit(solution)/shard_map/reduce_scatter | solution.py:73
  16.3 122.5 %reduce-scatter.7.cloned.1.call-start = ((), (), s32[]{:S(2)}) async-start(), calls=%async_computation.3 | async-start | bytes 589824
  118.8 89.5 %copy-start.1 = (f32[16,128]{1,0:T(8,128)}, f32[16,128]{1,0:T(8,128)S(1)}, u32[]{:S(2)}) copy-start(f32[16,128]{1,0:T(8,128)S(1)} %convolution_multiply_fusion) | copy-start | bytes 24580
Sparse Core Ops, SparseCore 0:
  16.4 56.5 reduce-scatter.4
  76.3 62.3 reduce-scatter.6
